TPU v7x, 32 devices: a whole 2x2x4 slice. The times are simulated.
32 devices in a mesh: region: 4 (over y, x), block: 8 (over z, core).
Axes of the slice: x: 2, y: 2, z: 4, core: 2. Of those that a mesh axis runs over, the one named last changes fastest.
Arguments:
- obs: bfloat16 [512, 32, 128], P(('region', 'block')), may hold values from -6 to 6
- predict: bfloat16 [512, 2, 128, 128], P(('region', 'block')), may hold values from -0.375 to 0.375
- factor: bfloat16 [512, 128, 128], P(('region', 'block')), as said below
- tau: float32 [32], replicated, may hold values from 0.5 to 2
- nbr_dev: int32 [512, 1], P(('region', 'block')), may hold values from 0 to 7; in each aligned block of 16 rows (0 to 15, 16 to 31, ...) at most 4 rows name the same one
- nbr_slot: int32 [512, 2], P(('region', 'block')), may hold values from 0 to 15
- counts: int32 [32], P(('region', 'block')), may hold values from 8 to 16
Outputs:
- grad_obs: float32 [512, 32, 128], P(('region', 'block'))
- grad_tau: float32 [32], replicated
Inputs may be any that keep to these rules, and one draw needn't show every extreme that they name: `nbr_dev`: among the blocks of one device at most 4 name the same device. `nbr_slot`: column 0 is a slot on the in-region neighbour's device, column 1 a slot on the device of the previous region with the same index along block. `factor`: each block's matrix is the identity plus small entries.
All inputs are finite; a program needn't handle non-finite values.
Results may differ from a plain program's by a relative error of at most 0.0035.
Values may be sent and summed in bfloat16 or wider, within the bound.
A program may use at most 64 MiB of HBM per device.

v0:
```python
import jax
import jax.numpy as jnp
from jax import lax
from jax.sharding import PartitionSpec as P


def passed_along(value, axis, steps):
    count = lax.axis_size(axis)
    leading, last = (max(0, -steps), min(count, count - steps))
    return lax.ppermute(value, axis, [(source, source + steps) for source in range(leading, last)])


def shards(obs, predict, factor, tau, nbr_dev, nbr_slot, counts):
    nbd = obs.shape[0]
    chans = obs.shape[1]
    width = obs.shape[2]
    nblock = lax.axis_size("block")
    cap_size = max(2, 2 * nbd // nblock)
    total_slots = nblock * cap_size
    dest = nbr_dev[:, 0]
    slot_one = nbr_slot[:, 0]
    slot_two = nbr_slot[:, 1]
    onehot = (dest[:, None] == jnp.arange(nblock, dtype=jnp.int32)[None, :]).astype(jnp.int32)
    before = jnp.cumsum(onehot, axis=0) - onehot
    rank_in = jnp.sum(before * onehot, axis=1)
    flat = dest * cap_size + rank_in
    match = (flat[:, None] == jnp.arange(total_slots, dtype=jnp.int32)[None, :]).astype(jnp.int32)
    filled = jnp.sum(match, axis=0)
    req_flat = jnp.sum(match * slot_one[:, None], axis=0) + (1 - filled) * nbd
    request = req_flat.reshape(nblock, cap_size)
    region_all = lax.all_gather(obs, "block", axis=0, tiled=True)
    near = jnp.take(region_all, dest * nbd + slot_one, axis=0)
    previous = passed_along(obs, "region", 1)
    far = jnp.take(previous, slot_two, axis=0)
    p_zero = predict[:, 0]
    p_one = predict[:, 1]
    err = obs.astype(jnp.float32) - jnp.einsum(
        "bcj,bjk->bck", near, p_zero, preferred_element_type=jnp.float32
    )
    err = err - jnp.einsum("bcj,bjk->bck", far, p_one, preferred_element_type=jnp.float32)
    err = err.astype(jnp.bfloat16)
    white = jnp.einsum("bcj,bjk->bck", err, factor, preferred_element_type=jnp.float32)
    live = (jnp.arange(nbd, dtype=jnp.int32) < counts[0]).astype(jnp.float32)
    weighted = (live[:, None, None] * tau[None, :, None] * white).astype(jnp.bfloat16)
    adj = jnp.einsum("bck,bjk->bcj", weighted, factor, preferred_element_type=jnp.float32)
    adj16 = adj.astype(jnp.bfloat16)
    back_one = -jnp.einsum("bck,bjk->bcj", adj16, p_zero, preferred_element_type=jnp.float32)
    back_two = -jnp.einsum("bck,bjk->bcj", adj16, p_one, preferred_element_type=jnp.float32)
    placed = jnp.einsum(
        "bs,bcj->scj", match.astype(jnp.float32), back_one, precision=lax.Precision.HIGHEST
    )
    placed = placed.reshape(nblock, cap_size, chans, width)
    returned, owned_slots = (
        lax.all_to_all(placed, "block", split_axis=0, concat_axis=0, tiled=True),
        lax.all_to_all(request, "block", split_axis=0, concat_axis=0, tiled=True),
    )
    spread = (owned_slots.reshape(-1)[:, None] == jnp.arange(nbd, dtype=jnp.int32)[None, :]).astype(
        jnp.float32
    )
    add_one = jnp.einsum(
        "sb,scj->bcj",
        spread,
        returned.reshape(total_slots, chans, width),
        precision=lax.Precision.HIGHEST,
    )
    seam_hot = (slot_two[:, None] == jnp.arange(nbd, dtype=jnp.int32)[None, :]).astype(jnp.float32)
    seam_dense = jnp.einsum("bs,bcj->scj", seam_hot, back_two, precision=lax.Precision.HIGHEST)
    add_two = passed_along(seam_dense, "region", -1)
    grad_obs = adj + add_one + add_two
    squares = jnp.sum(live[:, None, None] * white * white, axis=(0, 2))
    live_count = jnp.sum(live)
    total_sq, total_live = lax.psum((squares, live_count), ("region", "block"))
    all_blocks = nbd * lax.axis_size("region") * nblock
    grad_tau = (0.5 * total_sq - 0.5 * width * total_live / tau) / (all_blocks * width)
    return (grad_obs, grad_tau)


def solution(mesh):
    in_specs = (
        P(("region", "block"), None, None),
        P(("region", "block"), None, None, None),
        P(("region", "block"), None, None),
        P(),
        P(("region", "block"), None),
        P(("region", "block"), None),
        P(("region", "block")),
    )
    out_specs = (P(("region", "block"), None, None), P())
    return jax.shard_map(shards, mesh=mesh, in_specs=in_specs, out_specs=out_specs, check_vma=False)
```

profile of v0, /device:TPU:0, one launch (start us, length us, event | category | flops | bytes accessed | tf_op | source)
XLA Modules:
  0.0 102.5 jit_solution(590737278167899570)
XLA Ops:
  7.2 0.7 all-gather.2.cloned.1.call-update
  7.9 0.2 copy-done.2
  8.1 4.8 %collective-permute-start = (bf16[16,32,128]{2,1,0:T(8,128)(2,1)S(1)}, bf16[16,32,128]{2,1,0:T(8,128)(2,1)S(1)}, u32[]{:S(2)}, u32[]{:S(2)}) collective-permute-start(bf16[16,32,128]{2,1,0:T(8,128)(2,1)S(1)} %copy-done.2), channel_id=1, source_target_pairs={{0,8},{8,16},{16,24},{1,9},{9,17},{17,25},{2,10},{10,18},{18,26},{... | collective-permute-start | bytes 393224 | tf_op jit(solution)/shard_map/ppermute | solution.py:10
  13.0 0.7 fusion.33
  13.8 0.8 select_reduce_fusion.1
  14.6 0.8 slice_bitcast_fusion.1
  15.5 0.7 add.50
  16.1 4.9 %all-to-all-start = ((s32[8,1,4]{2,1,0:T(1,128)}), s32[8,1,4]{2,1,0:T(1,128)S(1)}, u32[]{:S(2)}, u32[]{:S(2)}) async-start(s32[8,1,4]{2,1,0:T(1,128)} %bitcast.11), calls=%async_computation | async-start | bytes 8192 | tf_op jit(solution)/shard_map/all_to_all | solution.py:55
  21.7 0.8 and_bitcast_fusion.1
  22.4 0.7 broadcast_multiply_fusion
  23.2 0.6 gather_fusion.1
  23.8 10.7 %all-gather.2.cloned.1.call-done = bf16[128,32,128]{2,1,0:T(8,128)(2,1)} async-done(((bf16[16,32,128]{2,1,0:T(8,128)(2,1)}), bf16[128,32,128]{2,1,0:T(8,128)(2,1)}) %all-gather.2.cloned.1.call-update) | async-done | bytes 1048592 | tf_op jit(solution)/shard_map/all_gather | solution.py:31
  34.5 1.8 %gather_fusion = bf16[16,32,128]{2,1,0:T(8,128)(2,1)S(1)} fusion(bf16[128,32,128]{2,1,0:T(8,128)(2,1)} %all-gather.2.cloned.1.call-done, s32[1024]{0:T(1024)S(1)} %pad_clamp_fusion.1), kind=kCustom, calls=%fused_computation | custom fusion | bytes 262208 | tf_op jit(solution)/shard_map/jit(_take)/gather | solution.py:32
  36.3 1.4 %convolution_subtract_fusion.1 = f32[16,32,128]{2,1,0:T(8,128)S(1)} fusion(bf16[16,2,128,128]{3,2,1,0:T(8,128)(2,1)} %param.8, bf16[16,32,128]{2,1,0:T(8,128)(2,1)S(1)} %copy-done.2, bf16[16,32,128]{2,1,0:T(8,128)(2,1)S(1)} %gather_fusion, pred[16]{0:T(512)(128)(4,1)S(1)} %get-tuple-element.6), kind=kOutput, calls=%fused_computation.5 | convolution fusion | flops 16973824 | bytes 1048592 | tf_op jit(solution)/shard_map/bcj,bjk->bck/dot_general | solution.py:37
  37.7 0.6 fusion.12
  38.2 0.4 fusion.18
  38.6 0.4 convolution_negate_fusion.1
  39.0 0.7 fusion.16
  39.8 0.9 copy.17
  40.7 3.5 %all-to-all-start.1 = ((f32[8,4,32,128]{3,1,2,0:T(4,128)}), f32[8,4,32,128]{3,1,2,0:T(4,128)S(1)}, u32[]{:S(2)}, u32[]{:S(2)}) async-start(f32[8,4,32,128]{3,1,2,0:T(4,128)} %copy.17), calls=%async_computation.1 | async-start | bytes 1048576 | tf_op jit(solution)/shard_map/all_to_all | solution.py:54
  44.2 0.6 fusion.47
  44.8 0.5 broadcast.119
  45.3 0.7 reduce.3
  46.0 0.4 convolution_negate_fusion
  46.4 0.4 fusion.13
  46.9 1.3 %collective-permute-start.1 = (f32[16,32,128]{2,1,0:T(8,128)S(1)}, f32[16,32,128]{2,1,0:T(8,128)S(1)}, u32[]{:S(2)}, u32[]{:S(2)}) collective-permute-start(f32[16,32,128]{2,1,0:T(8,128)S(1)} %copy.21), channel_id=1, source_target_pairs={{8,0},{16,8},{24,16},{9,1},{17,9},{25,17},{10,2},{18,10},{26,18},{... | collective-permute-start | bytes 786440 | tf_op jit(solution)/shard_map/ppermute | solution.py:10
  48.2 44.3 %all-reduce = (f32[32]{0:T(128)S(1)}, f32[]{:T(128)}) all-reduce(f32[32]{0:T(128)S(1)} %get-tuple-element.12, f32[]{:T(128)} %fusion.47), channel_id=1, replica_groups=mesh['region'=4,'block'=8] {'region','block'}, use_global_device_ids=true, to_apply=%region_5.6 | all-reduce | flops 33 | bytes 264 | tf_op jit(solution)/shard_map/psum | solution.py:72
  93.2 0.6 copy-done.3
  93.8 0.5 fusion.43
  94.3 0.1 copy.18
  94.5 0.3 fusion.35
  94.8 0.9 fusion.15
  (19 shorter events, 0.4 us)
Async XLA Ops:
  7.2 30.5 %copy-start = (bf16[16,128,128]{2,1,0:T(8,128)(2,1)S(1)}, bf16[16,128,128]{2,1,0:T(8,128)(2,1)}, u32[]{:S(2)}) copy-start(bf16[16,128,128]{2,1,0:T(8,128)(2,1)} %param.9) | copy-start | bytes 1572868
  7.2 1.0 copy-start.2
  7.2 30.5 %copy-start.1 = (bf16[16,2,128,128]{3,2,1,0:T(8,128)(2,1)S(1)}, bf16[16,2,128,128]{3,2,1,0:T(8,128)(2,1)}, u32[]{:S(2)}) copy-start(bf16[16,2,128,128]{3,2,1,0:T(8,128)(2,1)} %param.8) | copy-start | bytes 3145732
  7.2 27.3 %all-gather.2.cloned.1.call-start = ((), (), s32[]{:S(2)}) async-start(), calls=%async_computation.2 | async-start | bytes 1179648 | tf_op jit(solution)/shard_map/all_gather | solution.py:31
  8.1 15.0 %collective-permute-start = (bf16[16,32,128]{2,1,0:T(8,128)(2,1)S(1)}, bf16[16,32,128]{2,1,0:T(8,128)(2,1)S(1)}, u32[]{:S(2)}, u32[]{:S(2)}) collective-permute-start(bf16[16,32,128]{2,1,0:T(8,128)(2,1)S(1)} %copy-done.2), channel_id=1, source_target_pairs={{0,8},{8,16},{16,24},{1,9},{9,17},{17,25},{2,10},{10,18},{18,26},{... | collective-permute-start | bytes 393224 | tf_op jit(solution)/shard_map/ppermute | solution.py:10
  16.1 24.5 %all-to-all-start = ((s32[8,1,4]{2,1,0:T(1,128)}), s32[8,1,4]{2,1,0:T(1,128)S(1)}, u32[]{:S(2)}, u32[]{:S(2)}) async-start(s32[8,1,4]{2,1,0:T(1,128)} %bitcast.11), calls=%async_computation | async-start | bytes 8192 | tf_op jit(solution)/shard_map/all_to_all | solution.py:55
  40.7 53.7 %all-to-all-start.1 = ((f32[8,4,32,128]{3,1,2,0:T(4,128)}), f32[8,4,32,128]{3,1,2,0:T(4,128)S(1)}, u32[]{:S(2)}, u32[]{:S(2)}) async-start(f32[8,4,32,128]{3,1,2,0:T(4,128)} %copy.17), calls=%async_computation.1 | async-start | bytes 1048576 | tf_op jit(solution)/shard_map/all_to_all | solution.py:54
  46.9 47.9 %collective-permute-start.1 = (f32[16,32,128]{2,1,0:T(8,128)S(1)}, f32[16,32,128]{2,1,0:T(8,128)S(1)}, u32[]{:S(2)}, u32[]{:S(2)}) collective-permute-start(f32[16,32,128]{2,1,0:T(8,128)S(1)} %copy.21), channel_id=1, source_target_pairs={{8,0},{16,8},{24,16},{9,1},{17,9},{25,17},{10,2},{18,10},{26,18},{... | collective-permute-start | bytes 786440 | tf_op jit(solution)/shard_map/ppermute | solution.py:10
  93.1 0.7 copy-start.3
Sparse Core Ops, SparseCore 0:
  9.6 24.7 all-gather.1
where the time goes:
time: 103 us
  blocking collectives  44.3 us (43%)
  between operations  15.5 us (15%)
  starting transfers between devices  14.5 us (14%)
  waiting for transfers between devices  11.4 us (11%)
  other arithmetic  6.61 us (6%)
  local copies, waits for them, and re-layouts  5.62 us (5%)
  matrix products  4.57 us (4%)
    psum x1, blocking collectives, shards(): total_sq, total_live = lax.psum((squares, live_count), ('region', 'block'))  44.3 us
    all_gather x1, waiting for transfers between devices, shards(): region_all = lax.all_gather(obs, 'block', axis=0, tiled=True)  10.7 us
    ppermute x2, starting transfers between devices, passed_along(): lax.ppermute(value, axis, [(source, source + steps) for source in range(l...  6.13 us
    all_to_all x1, starting transfers between devices, shards(): lax.all_to_all(request, 'block', split_axis=0, concat_axis=0, tiled=True)  4.88 us
    all_to_all x1, starting transfers between devices, shards(): lax.all_to_all(placed, 'block', split_axis=0, concat_axis=0, tiled=True)  3.49 us
  transfers between devices with their start and end apart: 5, of which 1 were waited for; matrix products, arithmetic and copies ran while one was open for 15% of the time, Pallas kernels for 0%

commit v1 on v0

--- a/solution.py
+++ b/solution.py
@@ -2,6 +2,23 @@
 import jax.numpy as jnp
 from jax import lax
 from jax.sharding import PartitionSpec as P
+
+
+def joined_along(blocks, dim):
+    shape = list(blocks.shape[1:])
+    shape[dim] *= blocks.shape[0]
+    return jnp.moveaxis(blocks, 0, dim).reshape(shape)
+
+
+def gather_around(shard, axis, dim):
+    length = lax.axis_size(axis)
+    upward = [(i, (i + 1) % length) for i in range(length)]
+    pieces = [shard]
+    while len(pieces) < length:
+        pieces.append(lax.ppermute(pieces[-1], axis, upward))
+    index = lax.axis_index(axis)
+    pieces = jnp.stack(pieces)[(index - jnp.arange(length)) % length]
+    return joined_along(pieces, dim)
 
 
 def passed_along(value, axis, steps):
@@ -28,7 +45,7 @@
     filled = jnp.sum(match, axis=0)
     req_flat = jnp.sum(match * slot_one[:, None], axis=0) + (1 - filled) * nbd
     request = req_flat.reshape(nblock, cap_size)
-    region_all = lax.all_gather(obs, "block", axis=0, tiled=True)
+    region_all = gather_around(obs, "block", 0)
     near = jnp.take(region_all, dest * nbd + slot_one, axis=0)
     previous = passed_along(obs, "region", 1)
     far = jnp.take(previous, slot_two, axis=0)

time: 103 us -> 113 us (1.097)
  waiting for transfers between devices: 11.4 us -> 36 us
  between operations: 15.5 us -> 2.19 us
  other arithmetic: 6.61 us -> 3.16 us
  local copies, waits for them, and re-layouts: 5.62 us -> 8.64 us
    ppermute x0 -> x7, waiting for transfers between devices: none -> 35.9 us  [gather_around(): pieces.append(lax.ppermute(pieces[-1], axis, upward))]
    all_gather x1 -> x0, waiting for transfers between devices: 10.7 us -> none  [shards(): region_all = lax.all_gather(obs, 'block', axis=0, tiled=True)]
    gather x0 -> x1, local copies, waits for them, and re-layouts: none -> 1.67 us  [gather_around(): pieces = jnp.stack(pieces)[(index - jnp.arange(length)) % length]]
    unnamed x8 -> x19, local copies, waits for them, and re-layouts: 0.87 us -> 2.18 us
  transfers between devices with their start and end apart: 5 -> 11, of which waited for: 1 -> 6; matrix products, arithmetic and copies ran while one was open for 15% -> 12% of each run, Pallas kernels for 0% -> 0%
where the time goes in v1:
time: 113 us
  blocking collectives  44.3 us (39%)
  waiting for transfers between devices  36 us (32%)
  starting transfers between devices  15.3 us (14%)
  local copies, waits for them, and re-layouts  8.64 us (8%)
  matrix products  3.51 us (3%)
  other arithmetic  3.16 us (3%)
  between operations  2.19 us (2%)
    psum x1, blocking collectives, shards(): total_sq, total_live = lax.psum((squares, live_count), ('region', 'block'))  44.3 us
    ppermute x7, waiting for transfers between devices, gather_around(): pieces.append(lax.ppermute(pieces[-1], axis, upward))  35.9 us
    ppermute x2, starting transfers between devices, passed_along(): lax.ppermute(value, axis, [(source, source + steps) for source in range(l...  5.84 us
    all_to_all x1, starting transfers between devices, shards(): lax.all_to_all(request, 'block', split_axis=0, concat_axis=0, tiled=True)  4.88 us
    all_to_all x1, starting transfers between devices, shards(): lax.all_to_all(placed, 'block', split_axis=0, concat_axis=0, tiled=True)  3.49 us
  transfers between devices with their start and end apart: 11, of which 6 were waited for; matrix products, arithmetic and copies ran while one was open for 12% of the time, Pallas kernels for 0%

profile of v1, /device:TPU:0, one launch (start us, length us, event | category | flops | bytes accessed | tf_op | source)
XLA Modules:
  0.0 113.0 jit_solution(10701072475782666037)
XLA Ops:
  0.7 0.5 collective-permute-start
  1.2 4.5 %collective-permute-start.7 = (bf16[16,32,128]{2,1,0:T(8,128)(2,1)}, bf16[16,32,128]{2,1,0:T(8,128)(2,1)S(1)}, u32[]{:S(2)}, u32[]{:S(2)}) collective-permute-start(bf16[16,32,128]{2,1,0:T(8,128)(2,1)} %param.7), channel_id=1, source_target_pairs={{0,8},{8,16},{16,24},{1,9},{9,17},{17,25},{2,10},{10,18},{18,26},{... | collective-permute-start | bytes 393224 | tf_op jit(solution)/shard_map/ppermute | solution.py:27
  6.0 0.5 copy-done.4
  6.6 0.7 add.75
  7.3 4.9 %all-to-all-start = ((s32[8,1,4]{2,1,0:T(1,128)}), s32[8,1,4]{2,1,0:T(1,128)S(1)}, u32[]{:S(2)}, u32[]{:S(2)}) async-start(s32[8,1,4]{2,1,0:T(1,128)} %bitcast.21), calls=%async_computation | async-start | bytes 8192 | tf_op jit(solution)/shard_map/all_to_all | solution.py:72
  12.2 0.9 bitcast_dynamic-update-slice_fusion.7
  13.8 0.6 copy-done.5
  14.5 0.6 collective-permute-start.1
  15.1 0.6 gather_fusion.2
  15.7 5.1 %collective-permute-done.1 = bf16[16,32,128]{2,1,0:T(8,128)(2,1)S(1)} collective-permute-done((bf16[16,32,128]{2,1,0:T(8,128)(2,1)S(1)}, bf16[16,32,128]{2,1,0:T(8,128)(2,1)S(1)}, u32[]{:S(2)}, u32[]{:S(2)}) %collective-permute-start.1) | collective-permute-done | bytes 131104 | tf_op jit(solution)/shard_map/ppermute | solution.py:18
  20.9 6.2 %collective-permute-done.2 = bf16[16,32,128]{2,1,0:T(8,128)(2,1)S(1)} collective-permute-done((bf16[16,32,128]{2,1,0:T(8,128)(2,1)S(1)}, bf16[16,32,128]{2,1,0:T(8,128)(2,1)S(1)}, u32[]{:S(2)}, u32[]{:S(2)}) %collective-permute-start.2) | collective-permute-done | bytes 131104 | tf_op jit(solution)/shard_map/ppermute | solution.py:18
  27.0 6.2 %collective-permute-done.3 = bf16[16,32,128]{2,1,0:T(8,128)(2,1)S(1)} collective-permute-done((bf16[16,32,128]{2,1,0:T(8,128)(2,1)S(1)}, bf16[16,32,128]{2,1,0:T(8,128)(2,1)S(1)}, u32[]{:S(2)}, u32[]{:S(2)}) %collective-permute-start.3) | collective-permute-done | bytes 131104 | tf_op jit(solution)/shard_map/ppermute | solution.py:18
  33.2 6.2 %collective-permute-done.4 = bf16[16,32,128]{2,1,0:T(8,128)(2,1)S(1)} collective-permute-done((bf16[16,32,128]{2,1,0:T(8,128)(2,1)S(1)}, bf16[16,32,128]{2,1,0:T(8,128)(2,1)S(1)}, u32[]{:S(2)}, u32[]{:S(2)}) %collective-permute-start.4) | collective-permute-done | bytes 131104 | tf_op jit(solution)/shard_map/ppermute | solution.py:18
  39.4 6.2 %collective-permute-done.5 = bf16[16,32,128]{2,1,0:T(8,128)(2,1)S(1)} collective-permute-done((bf16[16,32,128]{2,1,0:T(8,128)(2,1)S(1)}, bf16[16,32,128]{2,1,0:T(8,128)(2,1)S(1)}, u32[]{:S(2)}, u32[]{:S(2)}) %collective-permute-start.5) | collective-permute-done | bytes 131104 | tf_op jit(solution)/shard_map/ppermute | solution.py:18
  45.6 6.2 %collective-permute-done.6 = bf16[16,32,128]{2,1,0:T(8,128)(2,1)S(1)} collective-permute-done((bf16[16,32,128]{2,1,0:T(8,128)(2,1)S(1)}, bf16[16,32,128]{2,1,0:T(8,128)(2,1)S(1)}, u32[]{:S(2)}, u32[]{:S(2)}) %collective-permute-start.6) | collective-permute-done | bytes 131104 | tf_op jit(solution)/shard_map/ppermute | solution.py:18
  51.8 1.7 %gather_fusion = bf16[8,16,32,128]{3,2,1,0:T(8,128)(2,1)} fusion(bf16[8,16,32,128]{3,2,1,0:T(8,128)(2,1)S(1)} %bitcast_dynamic-update-slice_fusion, s32[1024]{0:T(1024)S(1)} %pad_clamp_fusion.2), kind=kCustom, calls=%fused_computation | custom fusion | bytes 2097184 | tf_op jit(solution)/shard_map/gather | solution.py:20
  53.5 1.8 %gather_fusion.1 = bf16[16,32,128]{2,1,0:T(8,128)(2,1)S(1)} fusion(bf16[128,32,128]{2,1,0:T(8,128)(2,1)} %bitcast.74, s32[1024]{0:T(1024)S(1)} %pad_clamp_fusion.1), kind=kCustom, calls=%fused_computation.1 | custom fusion | bytes 262208 | tf_op jit(solution)/shard_map/jit(_take)/gather | solution.py:49
  55.7 0.6 fusion.12
  56.2 0.4 fusion.18
  56.6 0.4 convolution_negate_fusion.1
  57.0 0.7 fusion.16
  57.8 0.9 copy.17
  58.7 3.5 %all-to-all-start.1 = ((f32[8,4,32,128]{3,1,2,0:T(4,128)}), f32[8,4,32,128]{3,1,2,0:T(4,128)S(1)}, u32[]{:S(2)}, u32[]{:S(2)}) async-start(f32[8,4,32,128]{3,1,2,0:T(4,128)} %copy.17), calls=%async_computation.1 | async-start | bytes 1048576 | tf_op jit(solution)/shard_map/all_to_all | solution.py:71
  62.2 0.6 fusion.49
  62.8 0.5 broadcast.188
  63.3 0.7 reduce.3
  64.0 0.4 convolution_negate_fusion
  64.4 0.4 fusion.13
  64.9 1.3 %collective-permute-start.8 = (f32[16,32,128]{2,1,0:T(8,128)S(1)}, f32[16,32,128]{2,1,0:T(8,128)S(1)}, u32[]{:S(2)}, u32[]{:S(2)}) collective-permute-start(f32[16,32,128]{2,1,0:T(8,128)S(1)} %copy.21), channel_id=1, source_target_pairs={{8,0},{16,8},{24,16},{9,1},{17,9},{25,17},{10,2},{18,10},{26,18},{... | collective-permute-start | bytes 786440 | tf_op jit(solution)/shard_map/ppermute | solution.py:27
  66.2 44.3 %all-reduce = (f32[32]{0:T(128)S(1)}, f32[]{:T(128)}) all-reduce(f32[32]{0:T(128)S(1)} %get-tuple-element.12, f32[]{:T(128)} %fusion.49), channel_id=1, replica_groups=mesh['region'=4,'block'=8] {'region','block'}, use_global_device_ids=true, to_apply=%region_5.6 | all-reduce | flops 33 | bytes 264 | tf_op jit(solution)/shard_map/psum | solution.py:89
  111.2 0.5 fusion.45
  112.2 0.9 fusion.15
  (45 shorter events, 1.6 us)
Async XLA Ops:
  0.6 55.0 %copy-start = (bf16[16,128,128]{2,1,0:T(8,128)(2,1)S(1)}, bf16[16,128,128]{2,1,0:T(8,128)(2,1)}, u32[]{:S(2)}) copy-start(bf16[16,128,128]{2,1,0:T(8,128)(2,1)} %param.9) | copy-start | bytes 1572868
  0.6 5.1 %copy-start.3 = (s32[16,1]{0,1:T(1,128)S(1)}, s32[16,1]{0,1:T(1,128)}, u32[]{:S(2)}) copy-start(s32[16,1]{0,1:T(1,128)} %param.11) | copy-start | bytes 196
  0.7 13.9 %collective-permute-start = (bf16[16,32,128]{2,1,0:T(8,128)(2,1)}, bf16[16,32,128]{2,1,0:T(8,128)(2,1)S(1)}, u32[]{:S(2)}, u32[]{:S(2)}) collective-permute-start(bf16[16,32,128]{2,1,0:T(8,128)(2,1)} %param.7), channel_id=1, source_target_pairs={{0,1},{1,2},{2,3},{3,4},{4,5},{5,6},{6,7},{7,0},{8,9},{9,10},{10,1... | collective-permute-start | bytes 393224 | tf_op jit(solution)/shard_map/ppermute | solution.py:18
  1.2 13.9 %collective-permute-start.7 = (bf16[16,32,128]{2,1,0:T(8,128)(2,1)}, bf16[16,32,128]{2,1,0:T(8,128)(2,1)S(1)}, u32[]{:S(2)}, u32[]{:S(2)}) collective-permute-start(bf16[16,32,128]{2,1,0:T(8,128)(2,1)} %param.7), channel_id=1, source_target_pairs={{0,8},{8,16},{16,24},{1,9},{9,17},{17,25},{2,10},{10,18},{18,26},{... | collective-permute-start | bytes 393224 | tf_op jit(solution)/shard_map/ppermute | solution.py:27
  5.8 0.7 copy-start.4
  7.3 51.4 %all-to-all-start = ((s32[8,1,4]{2,1,0:T(1,128)}), s32[8,1,4]{2,1,0:T(1,128)S(1)}, u32[]{:S(2)}, u32[]{:S(2)}) async-start(s32[8,1,4]{2,1,0:T(1,128)} %bitcast.21), calls=%async_computation | async-start | bytes 8192 | tf_op jit(solution)/shard_map/all_to_all | solution.py:72
  13.8 0.7 copy-start.5
  14.5 6.3 %collective-permute-start.1 = (bf16[16,32,128]{2,1,0:T(8,128)(2,1)S(1)}, bf16[16,32,128]{2,1,0:T(8,128)(2,1)S(1)}, u32[]{:S(2)}, u32[]{:S(2)}) collective-permute-start(bf16[16,32,128]{2,1,0:T(8,128)(2,1)S(1)} %collective-permute-done), channel_id=1, source_target_pairs={{0,1},{1,2},{2,3},{3,4},{4,5},{5,6},{6,7},{7,0},{8,9},{9,10},{10,1... | collective-permute-start | bytes 393224 | tf_op jit(solution)/shard_map/ppermute | solution.py:18
  20.8 6.2 %collective-permute-start.2 = (bf16[16,32,128]{2,1,0:T(8,128)(2,1)S(1)}, bf16[16,32,128]{2,1,0:T(8,128)(2,1)S(1)}, u32[]{:S(2)}, u32[]{:S(2)}) collective-permute-start(bf16[16,32,128]{2,1,0:T(8,128)(2,1)S(1)} %collective-permute-done.1), channel_id=1, source_target_pairs={{0,1},{1,2},{2,3},{3,4},{4,5},{5,6},{6,7},{7,0},{8,9},{9,10},{10,1... | collective-permute-start | bytes 393224 | tf_op jit(solution)/shard_map/ppermute | solution.py:18
  27.0 6.2 %collective-permute-start.3 = (bf16[16,32,128]{2,1,0:T(8,128)(2,1)S(1)}, bf16[16,32,128]{2,1,0:T(8,128)(2,1)S(1)}, u32[]{:S(2)}, u32[]{:S(2)}) collective-permute-start(bf16[16,32,128]{2,1,0:T(8,128)(2,1)S(1)} %collective-permute-done.2), channel_id=1, source_target_pairs={{0,1},{1,2},{2,3},{3,4},{4,5},{5,6},{6,7},{7,0},{8,9},{9,10},{10,1... | collective-permute-start | bytes 393224 | tf_op jit(solution)/shard_map/ppermute | solution.py:18
  33.2 6.2 %collective-permute-start.4 = (bf16[16,32,128]{2,1,0:T(8,128)(2,1)S(1)}, bf16[16,32,128]{2,1,0:T(8,128)(2,1)S(1)}, u32[]{:S(2)}, u32[]{:S(2)}) collective-permute-start(bf16[16,32,128]{2,1,0:T(8,128)(2,1)S(1)} %collective-permute-done.3), channel_id=1, source_target_pairs={{0,1},{1,2},{2,3},{3,4},{4,5},{5,6},{6,7},{7,0},{8,9},{9,10},{10,1... | collective-permute-start | bytes 393224 | tf_op jit(solution)/shard_map/ppermute | solution.py:18
  39.4 6.2 %collective-permute-start.5 = (bf16[16,32,128]{2,1,0:T(8,128)(2,1)S(1)}, bf16[16,32,128]{2,1,0:T(8,128)(2,1)S(1)}, u32[]{:S(2)}, u32[]{:S(2)}) collective-permute-start(bf16[16,32,128]{2,1,0:T(8,128)(2,1)S(1)} %collective-permute-done.4), channel_id=1, source_target_pairs={{0,1},{1,2},{2,3},{3,4},{4,5},{5,6},{6,7},{7,0},{8,9},{9,10},{10,1... | collective-permute-start | bytes 393224 | tf_op jit(solution)/shard_map/ppermute | solution.py:18
  45.6 6.2 %collective-permute-start.6 = (bf16[16,32,128]{2,1,0:T(8,128)(2,1)S(1)}, bf16[16,32,128]{2,1,0:T(8,128)(2,1)S(1)}, u32[]{:S(2)}, u32[]{:S(2)}) collective-permute-start(bf16[16,32,128]{2,1,0:T(8,128)(2,1)S(1)} %collective-permute-done.5), channel_id=1, source_target_pairs={{0,1},{1,2},{2,3},{3,4},{4,5},{5,6},{6,7},{7,0},{8,9},{9,10},{10,1... | collective-permute-start | bytes 393224 | tf_op jit(solution)/shard_map/ppermute | solution.py:18
  51.8 3.5 %copy-start.1 = (bf16[16,2,128,128]{3,2,1,0:T(8,128)(2,1)S(1)}, bf16[16,2,128,128]{3,2,1,0:T(8,128)(2,1)}, u32[]{:S(2)}) copy-start(bf16[16,2,128,128]{3,2,1,0:T(8,128)(2,1)} %param.8) | copy-start | bytes 3145732
  53.5 1.9 %copy-start.2 = (bf16[16,32,128]{2,1,0:T(8,128)(2,1)S(1)}, bf16[16,32,128]{2,1,0:T(8,128)(2,1)}, u32[]{:S(2)}) copy-start(bf16[16,32,128]{2,1,0:T(8,128)(2,1)} %param.7) | copy-start | bytes 393220
  58.7 53.0 %all-to-all-start.1 = ((f32[8,4,32,128]{3,1,2,0:T(4,128)}), f32[8,4,32,128]{3,1,2,0:T(4,128)S(1)}, u32[]{:S(2)}, u32[]{:S(2)}) async-start(f32[8,4,32,128]{3,1,2,0:T(4,128)} %copy.17), calls=%async_computation.1 | async-start | bytes 1048576 | tf_op jit(solution)/shard_map/all_to_all | solution.py:71
  64.9 47.2 %collective-permute-start.8 = (f32[16,32,128]{2,1,0:T(8,128)S(1)}, f32[16,32,128]{2,1,0:T(8,128)S(1)}, u32[]{:S(2)}, u32[]{:S(2)}) collective-permute-start(f32[16,32,128]{2,1,0:T(8,128)S(1)} %copy.21), channel_id=1, source_target_pairs={{8,0},{16,8},{24,16},{9,1},{17,9},{25,17},{10,2},{18,10},{26,18},{... | collective-permute-start | bytes 786440 | tf_op jit(solution)/shard_map/ppermute | solution.py:27
